TPU v7x, 32 devices: a whole 2x2x4 slice. The times are simulated.
32 devices in a mesh: groups: 2 (over y), adapter: 4 (over x, core), mp: 4 (over z).
Axes of the slice: x: 2, y: 2, z: 4, core: 2. Of those that a mesh axis runs over, the one named last changes fastest.
Arguments:
- hidden: bfloat16 [3072, 16384], P(('groups', 'adapter'), 'mp'), parts along dimension 0, may hold values from -6 to 6
- adapter_ids: int32 [3072], P(('groups', 'adapter')), parts along dimension 0, may hold values from 0 to 7, as said below
- down_weight: bfloat16 [16384, 4096], P('mp'), may hold values from -0.0625 to 0.0625
- adapter_down: bfloat16 [16, 64, 16384], P(('groups', 'adapter'), None, 'mp'), parts along dimension 0, may hold values from -6 to 6
- adapter_up: bfloat16 [16, 64, 4096], P(('groups', 'adapter'), None, 'mp'), parts along dimension 0, may hold values from -6 to 6
- migration_plan: int32 [16], P(('groups', 'adapter')), parts along dimension 0, may hold values from 0 to 7, each once
Outputs:
- layer_result: bfloat16 [3072, 4096], P(('groups', 'adapter'), 'mp'), parts along dimension 0
- moved_down: bfloat16 [16, 64, 16384], P(('groups', 'adapter'), None, 'mp'), parts along dimension 0
- moved_up: bfloat16 [16, 64, 4096], P(('groups', 'adapter'), None, 'mp'), parts along dimension 0
There are 2 independent parts, one for each index of `groups`. A program takes and returns all parts, laid end to end along the dimension named above; an argument that names none is the same for every part. Nothing has to cross between parts.
Inputs may be any that keep to these rules, and one draw needn't show every extreme that they name: `adapter_ids`: among the 384 requests of one index of adapter, at most 192 ask for one adapter; in every draw one adapter is asked for by exactly 192 requests of every index. `migration_plan`: each adapter appears exactly once.
All inputs are finite; a program needn't handle non-finite values.
Results may differ from a plain program's by a relative error of at most 0.012.
Values may be sent and summed in bfloat16 or wider, within the bound.
A program may use at most 128 MiB of HBM per device.

v0:
```python
import math

import jax
import jax.numpy as jnp
from jax import lax
from jax.sharding import PartitionSpec as P

FF = 16384
RANK = 64


def per_device(hidden, adapter_ids, down_weight, adapter_down, adapter_up, migration_plan):
    row_count = hidden.shape[0]
    owners = lax.axis_size("adapter")
    local_count = adapter_down.shape[0]
    output_width = adapter_up.shape[2]
    adapter_grand_sum = local_count * owners
    inv_units = 1.0 / math.sqrt(FF)
    out_scale = 0.5 / math.sqrt(RANK)
    store_down, store_up = (
        lax.all_gather(adapter_down, "adapter", axis=0, tiled=True),
        lax.all_gather(adapter_up, "adapter", axis=0, tiled=True),
    )
    moved_down = store_down[migration_plan]
    moved_up = store_up[migration_plan]
    product = jnp.dot(hidden, down_weight, preferred_element_type=jnp.float32)
    base_product = lax.psum_scatter(
        jnp.transpose(
            product.reshape(row_count, 1 * lax.axis_size("mp"), output_width), (1, 0, 2)
        ).astype(jnp.bfloat16),
        "mp",
        scatter_dimension=0,
        tiled=True,
    ).astype(jnp.float32)[0]
    catalog = jnp.arange(adapter_grand_sum, dtype=jnp.int32)
    matches = adapter_ids[:, None] == catalog[None, :]
    selector = matches.astype(jnp.float32)
    all_factors = jnp.einsum("rf,jqf->jqr", hidden, store_down, preferred_element_type=jnp.float32)
    factor = jnp.sum(all_factors * jnp.transpose(selector)[:, None, :], axis=0)
    factor = lax.psum(factor.astype(jnp.bfloat16), "mp").astype(jnp.float32)
    factor = (factor * inv_units).astype(jnp.bfloat16)
    spread = jnp.einsum("qr,jqc->rjc", factor, store_up, preferred_element_type=jnp.float32)
    low_rank_change = (jnp.sum(spread * selector[:, :, None], axis=1) * out_scale).astype(
        jnp.bfloat16
    )
    layer_result = (base_product + low_rank_change.astype(jnp.float32)).astype(jnp.bfloat16)
    return (layer_result, moved_down, moved_up)


def solution(mesh):
    placed = (
        P(("groups", "adapter"), "mp"),
        P(("groups", "adapter")),
        P("mp", None),
        P(("groups", "adapter"), None, "mp"),
        P(("groups", "adapter"), None, "mp"),
        P(("groups", "adapter")),
    )
    return jax.shard_map(
        per_device,
        mesh=mesh,
        in_specs=placed,
        out_specs=(
            P(("groups", "adapter"), "mp"),
            P(("groups", "adapter"), None, "mp"),
            P(("groups", "adapter"), None, "mp"),
        ),
        check_vma=False,
    )
```

profile of v0, /device:TPU:0, one launch (start us, length us, event | category | flops | bytes accessed | tf_op | source)
XLA Modules:
  0.0 110.5 jit_solution(14232182022946486478)
XLA Ops:
  8.0 0.0 copy-start
  8.0 0.0 all-gather.5.cloned.1.call-start
  8.1 0.7 all-gather.5.cloned.1.call-update
  8.7 0.0 all-gather.3.cloned.1.call-start
  8.8 0.7 all-gather.3.cloned.1.call-update
  9.5 0.0 reduce-scatter.2.cloned.1.call-start
  9.5 0.3 copy-done
  9.9 19.1 %convolution_convert_fusion = bf16[384,4096]{1,0:T(8,128)(2,1)S(1)} fusion(bf16[384,4096]{1,0:T(8,128)(2,1)S(1)} %copy-done, bf16[4096,4096]{1,0:T(8,128)(2,1)} %param.8), kind=kOutput, calls=%fused_computation.3 | convolution fusion | flops 12886474752 | bytes 39845888 | tf_op jit(solution)/shard_map/dot_general | solution.py:26
  29.0 2.0 %copy.14 = bf16[48,4,8,1024]{3,2,0,1:T(8,128)(2,1)} copy(bf16[48,4,8,1024]{3,2,1,0:T(8,128)(2,1)S(1)} %bitcast.25) | data formatting | bytes 6291456 | tf_op jit(solution)/shard_map/convert_element_type | solution.py:30
  31.0 0.0 copy-start.2
  31.0 0.0 copy-start.1
  31.0 0.0 reduce-scatter.2.cloned.1.call-update
  31.0 0.6 copy-done.2
  31.6 0.0 copy-done.1
  31.7 0.0 all-gather.5.cloned.1.call-done
  31.7 2.5 %gather_fusion.1 = bf16[2,64,1024]{2,1,0:T(8,128)(2,1)} fusion(bf16[8,64,1024]{2,1,0:T(8,128)(2,1)} %all-gather.5.cloned.1.call-done, s32[1024]{0:T(1024)S(1)} %pad_clamp_fusion), kind=kCustom, calls=%fused_computation.1 | custom fusion | bytes 524296 | tf_op jit(solution)/shard_map/gather | solution.py:25
  34.2 31.8 %all-gather.3.cloned.1.call-done = bf16[8,64,4096]{2,1,0:T(8,128)(2,1)} async-done(((bf16[2,64,4096]{2,1,0:T(8,128)(2,1)}), bf16[8,64,4096]{2,1,0:T(8,128)(2,1)}) %all-gather.3.cloned.1.call-update) | async-done | bytes 4194320 | tf_op jit(solution)/shard_map/all_gather | solution.py:21
  66.0 3.8 %gather_fusion = bf16[2,64,4096]{2,1,0:T(8,128)(2,1)} fusion(bf16[8,64,4096]{2,1,0:T(8,128)(2,1)} %all-gather.3.cloned.1.call-done, s32[1024]{0:T(1024)S(1)} %pad_clamp_fusion), kind=kCustom, calls=%fused_computation | custom fusion | bytes 2097160 | tf_op jit(solution)/shard_map/gather | solution.py:24
  69.8 4.6 %fusion.6 = bf16[64,384]{1,0:T(8,128)(2,1)S(1)} fusion(bf16[8,64,4096]{2,1,0:T(8,128)(2,1)} %all-gather.3.cloned.1.call-done, bf16[384,4096]{1,0:T(8,128)(2,1)S(1)} %copy-done, f32[8,384]{1,0:T(8,128)S(1)} %fusion.12), kind=kOutput, calls=%fused_computation.11 | convolution fusion | flops 1610981376 | bytes 7401472 | tf_op jit(solution)/shard_map/rf,jqf->jqr/dot_general | solution.py:38
  74.3 21.6 %psum.7 = bf16[64,384]{1,0:T(8,128)(2,1)S(1)} all-reduce(bf16[64,384]{1,0:T(8,128)(2,1)S(1)} %fusion.6), channel_id=1, replica_groups=mesh['groups'=2,'adapter'=4,'mp'=4] {'mp'}, use_global_device_ids=true, to_apply=%region_2.0 | all-reduce | flops 24576 | bytes 98304 | tf_op jit(solution)/shard_map/psum | solution.py:40
  96.0 4.3 %multiply_reduce_fusion = f32[384,1024]{1,0:T(8,128)} fusion(f32[384,8]{0,1:T(8,128)S(1)} %fusion.13, bf16[8,64,1024]{2,1,0:T(8,128)(2,1)} %all-gather.5.cloned.1.call-done, bf16[64,384]{1,0:T(8,128)(2,1)S(1)} %psum.7), kind=kOutput, calls=%fused_computation.2 | convolution fusion | flops 408625152 | bytes 2682880 | tf_op jit(solution)/shard_map/qr,jqc->rjc/dot_general | solution.py:42
  100.3 0.0 reduce-scatter.2.cloned.1.call-done
  100.3 2.7 %fusion.2 = bf16[384,1024]{1,0:T(8,128)(2,1)} fusion(f32[384,1024]{1,0:T(8,128)} %multiply_reduce_fusion, bf16[1,384,1024]{2,1,0:T(8,128)(2,1)} %reduce-scatter.2.cloned.1.call-done), kind=kLoop, calls=%fused_computation.8 | loop fusion | flops 2359296 | bytes 3145728 | tf_op jit(solution)/shard_map/convert_element_type | solution.py:46
  (4 shorter events, 0.0 us)
Async XLA Ops:
  8.0 1.9 %copy-start = (bf16[384,4096]{1,0:T(8,128)(2,1)S(1)}, bf16[384,4096]{1,0:T(8,128)(2,1)}, u32[]{:S(2)}) copy-start(bf16[384,4096]{1,0:T(8,128)(2,1)} %param.6) | copy-start | bytes 9437188
  8.0 23.7 %all-gather.5.cloned.1.call-start = ((), (), s32[]{:S(2)}) async-start(), calls=%async_computation.3 | async-start | bytes 1310720 | tf_op jit(solution)/shard_map/all_gather | solution.py:22
  8.7 57.2 %all-gather.3.cloned.1.call-start = ((), (), s32[]{:S(2)}) async-start(), calls=%async_computation.2 | async-start | bytes 5242880 | tf_op jit(solution)/shard_map/all_gather | solution.py:21
  9.5 90.8 %reduce-scatter.2.cloned.1.call-start = ((), (), s32[]{:S(2)}) async-start(), calls=%async_computation.1 | async-start | bytes 3932160 | tf_op jit(solution)/shard_map/reduce_scatter | solution.py:27
  31.0 0.7 copy-start.2
  31.0 0.7 copy-start.1
Sparse Core Ops, SparseCore 0:
  10.4 19.4 all-gather.4
  31.4 34.5 all-gather.2
Sparse Core Ops, SparseCore 1:
  31.1 64.4 reduce-scatter.1
where the time goes:
time: 111 us; the launch traced here: 110 us
  waiting for transfers between devices  33.2 us (30%)
  matrix products  28 us (25%)
  blocking collectives  21.6 us (19%)
  between operations  15.5 us (14%)
  local copies, waits for them, and re-layouts  9.26 us (8%)
  other arithmetic  2.76 us (2%)
    all_gather x1, waiting for transfers between devices, per_device(): lax.all_gather(adapter_down, 'adapter', axis=0, tiled=True)  31.8 us
    psum x1, blocking collectives, per_device(): factor = lax.psum(factor.astype(jnp.bfloat16), 'mp').astype(jnp.float32)  21.6 us
    dot_general x1, matrix products, per_device(): product = jnp.dot(hidden, down_weight, preferred_element_type=jnp.float32)  19.1 us
    dot_general x1, matrix products, per_device(): jnp.einsum('rf,jqf->jqr', hidden, store_down, preferred_element_type=jnp....  4.58 us
    dot_general x1, matrix products, per_device(): jnp.einsum('qr,jqc->rjc', factor, store_up, preferred_element_type=jnp.fl...  4.32 us
    gather x1, local copies, waits for them, and re-layouts, per_device(): moved_down = store_down[migration_plan]  3.78 us
    convert_element_type x1, other arithmetic, per_device(): (base_product + low_rank_change.astype(jnp.float32)).astype(jnp.bfloat16)  2.74 us
    gather x1, local copies, waits for them, and re-layouts, per_device(): moved_up = store_up[migration_plan]  2.49 us
  transfers between devices with their start and end apart: 3, of which 1 were waited for; matrix products, arithmetic and copies ran while one was open for 33% of the time, Pallas kernels for 0%

commit v1 on v0

v1 whole, which is shorter than its diff:
```python
import functools
import math

import jax
import jax.numpy as jnp
from jax import lax
from jax.experimental import pallas as pl
from jax.experimental.pallas import tpu as pltpu
from jax.sharding import PartitionSpec as P

MESH = pl.DeviceIdType.MESH
SLOTS = 3
STRIDE = 3


def kernel(
    n, na, tile, inv_units, out_scale,
    plan_ref, hidden_ref, ids_ref, down_ref, up_ref, weight_ref,
    out_ref, mdown_ref, mup_ref,
    weights, prod, recv, store_down, store_up, fac, lora, spread, total,
    w_sem, z_send, z_recv, local_sem, x_send, x_recv, f_send, f_recv,
):
    me = lax.axis_index("mp")
    ad = lax.axis_index("adapter")
    rows = hidden_ref.shape[0]
    width = out_ref.shape[1]
    tiles = width // tile
    count = n * tiles
    local_count, rank, _ = mdown_ref.shape
    before, after = me, n - 1 - me
    far, near = jnp.maximum(before, after), jnp.minimum(before, after)
    lone = far - near
    right_far = (after > before).astype(jnp.int32)

    def visit(s):
        t = jnp.maximum(s - lone, 0)
        k = jnp.where(s < lone, far - s, near - t // 2)
        on_far = jnp.where(s < lone, 1, t % 2)
        right = jnp.where(on_far == 1, right_far, 1 - right_far)
        return me + jnp.where(right == 1, k, -k), right

    def weight_copy(t, slot):
        d, _ = visit(t // tiles)
        col = pl.multiple_of(d * width + (t % tiles) * tile, tile)
        return pltpu.make_async_copy(
            weight_ref.at[:, pl.ds(col, tile)], weights.at[slot], w_sem.at[slot]
        )

    for t in range(SLOTS - 1):
        weight_copy(t, t).start()
    own_down = pltpu.make_async_copy(down_ref, store_down.at[ad], local_sem.at[0])
    own_up = pltpu.make_async_copy(up_ref, store_up.at[ad], local_sem.at[1])
    own_down.start()
    own_up.start()

    bits = []
    bit = na // 2
    while bit:
        bits.append(bit)
        bit //= 2

    def partner(b):
        return ad + jnp.where((ad // b) % 2 == 1, -b, b)

    def slot_of(s):
        x = ad
        for b in bits:
            if s & b:
                x = x + jnp.where((ad // b) % 2 == 1, -b, b)
        return x

    barrier = pltpu.get_barrier_semaphore()

    @pl.loop(1, n)
    def _(i):
        pl.semaphore_signal(
            barrier, inc=1, device_id={"mp": (me + i) % n}, device_id_type=MESH
        )

    for b in bits:
        pl.semaphore_signal(
            barrier, inc=1, device_id={"adapter": partner(b)}, device_id_type=MESH
        )
    pl.semaphore_wait(barrier, n - 1 + len(bits))

    def adapter_copies(b, s):
        slot = slot_of(s)
        out = []
        for i, (mine, store) in enumerate(((down_ref, store_down), (up_ref, store_up))):
            out.append(
                pltpu.make_async_remote_copy(
                    src_ref=mine if s == 0 else store.at[slot],
                    dst_ref=store.at[slot],
                    send_sem=x_send.at[i, b ^ s],
                    recv_sem=x_recv.at[i, b ^ s],
                    device_id={"adapter": partner(b)},
                    device_id_type=MESH,
                )
            )
        return out

    for b in bits:
        for c in adapter_copies(b, 0):
            c.start()

    def block_copy(d, right, j):
        return pltpu.make_async_remote_copy(
            src_ref=prod.at[d, j],
            dst_ref=recv.at[right, d, j],
            send_sem=z_send.at[d, j],
            recv_sem=z_recv.at[right, d, j],
            device_id={"mp": jnp.where(right == 1, (me + 1) % n, (me + n - 1) % n)},
            device_id_type=MESH,
        )

    def first_in_line(right):
        return jnp.where(right == 1, before, after) == 0

    def forward(item):
        d, right = visit(item // tiles)
        j = item % tiles

        @pl.when(jnp.logical_not(first_in_line(right)))
        def _():
            copy = block_copy(d, right, j)
            copy.wait_recv()
            prod[d, j] = (
                prod[d, j].astype(jnp.float32) + recv[right, d, j].astype(jnp.float32)
            ).astype(jnp.bfloat16)
            copy.start()

    start_forward = tiles + 1
    early = max(0, min(-(-(count - start_forward) // STRIDE), (n - 2) * tiles))

    @pl.loop(0, count)
    def _(t):
        slot = t % SLOTS

        @pl.when(t + SLOTS - 1 < count)
        def _():
            weight_copy(t + SLOTS - 1, (t + SLOTS - 1) % SLOTS).start()

        weight_copy(t, slot).wait()
        d, right = visit(t // tiles)
        j = t % tiles
        prod[d, j] = jnp.dot(
            hidden_ref[...], weights[slot], preferred_element_type=jnp.float32
        ).astype(jnp.bfloat16)

        @pl.when(jnp.logical_and(d != me, first_in_line(right)))
        def _():
            block_copy(d, right, j).start()

        if early:
            step = t - start_forward

            @pl.when((step >= 0) & (step % STRIDE == 0) & (step < early * STRIDE))
            def _():
                forward(jnp.maximum(step, 0) // STRIDE)

    @pl.loop(early, (n - 2) * tiles)
    def _(i):
        forward(i)

    held = [0]
    for b in bits:
        for s in held:
            if s:
                for c in adapter_copies(b, s):
                    c.start()
        if b == bits[-1]:

            @pl.loop((n - 2) * tiles, (n - 1) * tiles)
            def _(i):
                forward(i)

        for s in held:
            for c in adapter_copies(b, s):
                c.wait_recv()
        held = held + [s ^ b for s in held]

    own_down.wait()
    own_up.wait()

    total_adapters = na * local_count
    stacked = store_down[...].reshape(total_adapters * rank, store_down.shape[2])
    every = lax.dot_general(
        stacked, hidden_ref[...], (((1,), (1,)), ((), ())), preferred_element_type=jnp.float32
    )
    ids = ids_ref[...]
    part = jnp.zeros((rank, rows), jnp.float32)
    for g in range(total_adapters):
        part = part + jnp.where(ids == g, every[g * rank : (g + 1) * rank], 0.0)
    fac[me] = part.astype(jnp.bfloat16)

    def factor_copy(source, target):
        return pltpu.make_async_remote_copy(
            src_ref=fac.at[source],
            dst_ref=fac.at[source],
            send_sem=f_send.at[target],
            recv_sem=f_recv.at[source],
            device_id={"mp": target},
            device_id_type=MESH,
        )

    @pl.loop(1, n)
    def _(i):
        factor_copy(me, (me + i) % n).start()

    for s in range(local_count):
        g = plan_ref[s]
        mdown_ref[s] = store_down[g // local_count, pl.ds((g % local_count) * rank, rank), :]
        mup_ref[s] = store_up[g // local_count, pl.ds((g % local_count) * rank, rank), :]

    @pl.loop(1, n)
    def _(i):
        other = (me + i) % n
        factor_copy(other, other).wait_recv()

    factor = fac[0].astype(jnp.float32)
    for i in range(1, n):
        factor = factor + fac[i].astype(jnp.float32)
    factor = (factor * inv_units).astype(jnp.bfloat16).astype(jnp.float32)
    for g in range(total_adapters):
        spread[g * rank : (g + 1) * rank, :] = jnp.where(ids == g, factor, 0.0).astype(
            jnp.bfloat16
        )
    turned = jnp.transpose(spread[...].astype(jnp.float32)).astype(jnp.bfloat16)
    for j in range(tiles):
        cols = slice(j * tile, (j + 1) * tile)
        lora[:, cols] = (
            jnp.dot(
                turned,
                store_up[:, :, cols].reshape(total_adapters * rank, tile),
                preferred_element_type=jnp.float32,
            )
            * out_scale
        ).astype(jnp.bfloat16)

    for j in range(tiles):
        cols = slice(j * tile, (j + 1) * tile)
        total[...] = prod[me, j].astype(jnp.float32)
        for right, there in ((1, before > 0), (0, after > 0)):

            @pl.when(there)
            def _(right=right, j=j):
                block_copy(me, jnp.int32(right), j).wait_recv()
                total[...] += recv[right, me, j].astype(jnp.float32)

        out_ref[:, cols] = (total[...] + lora[:, cols].astype(jnp.float32)).astype(jnp.bfloat16)

    @pl.loop(0, (n - 1) * tiles)
    def _(i):
        d, right = visit(i // tiles)
        block_copy(d, right, i % tiles).wait_send()

    @pl.loop(1, n)
    def _(i):
        factor_copy(me, (me + i) % n).wait_send()

    held = [0]
    for b in bits:
        for s in held:
            for c in adapter_copies(b, s):
                c.wait_send()
        held = held + [s ^ b for s in held]


def per_device(n, na, hidden, adapter_ids, down_weight, adapter_down, adapter_up, migration_plan):
    rows, units = hidden.shape
    local_count, rank, width = adapter_up.shape
    tile = min(256, width)
    tiles = width // tile
    stack = local_count * rank
    vmem = pl.BlockSpec(memory_space=pltpu.VMEM)
    bf16 = jnp.bfloat16
    result, moved_down, moved_up = pl.pallas_call(
        functools.partial(
            kernel, n, na, tile, 1.0 / math.sqrt(units * n), 0.5 / math.sqrt(rank)
        ),
        out_shape=(
            jax.ShapeDtypeStruct((rows, width), bf16),
            jax.ShapeDtypeStruct(adapter_down.shape, bf16),
            jax.ShapeDtypeStruct(adapter_up.shape, bf16),
        ),
        in_specs=[pl.BlockSpec(memory_space=pltpu.SMEM), vmem, vmem, vmem, vmem]
        + [pl.BlockSpec(memory_space=pl.ANY)],
        out_specs=(vmem, vmem, vmem),
        scratch_shapes=[
            pltpu.VMEM((SLOTS, units, tile), bf16),
            pltpu.VMEM((n, tiles, rows, tile), bf16),
            pltpu.VMEM((2, n, tiles, rows, tile), bf16),
            pltpu.VMEM((na, stack, units), bf16),
            pltpu.VMEM((na, stack, width), bf16),
            pltpu.VMEM((n, rank, rows), bf16),
            pltpu.VMEM((rows, width), bf16),
            pltpu.VMEM((na * stack, rows), bf16),
            pltpu.VMEM((rows, tile), jnp.float32),
            pltpu.SemaphoreType.DMA((SLOTS,)),
            pltpu.SemaphoreType.DMA((n, tiles)),
            pltpu.SemaphoreType.DMA((2, n, tiles)),
            pltpu.SemaphoreType.DMA((2,)),
            pltpu.SemaphoreType.DMA((2, na)),
            pltpu.SemaphoreType.DMA((2, na)),
            pltpu.SemaphoreType.DMA((n,)),
            pltpu.SemaphoreType.DMA((n,)),
        ],
        compiler_params=pltpu.CompilerParams(
            collective_id=0, has_side_effects=True, vmem_limit_bytes=56 << 20
        ),
    )(
        migration_plan,
        hidden,
        adapter_ids[None, :],
        adapter_down.reshape(stack, units),
        adapter_up.reshape(stack, width),
        down_weight,
    )
    return result, moved_down, moved_up


def solution(mesh):
    placed = (
        P(("groups", "adapter"), "mp"),
        P(("groups", "adapter")),
        P("mp", None),
        P(("groups", "adapter"), None, "mp"),
        P(("groups", "adapter"), None, "mp"),
        P(("groups", "adapter")),
    )
    return jax.shard_map(
        functools.partial(per_device, mesh.shape["mp"], mesh.shape["adapter"]),
        mesh=mesh,
        in_specs=placed,
        out_specs=(
            P(("groups", "adapter"), "mp"),
            P(("groups", "adapter"), None, "mp"),
            P(("groups", "adapter"), None, "mp"),
        ),
        check_vma=False,
    )
```

time: 111 us -> 74.6 us (0.67)
  Pallas kernels: 0 us -> 66.5 us
  waiting for transfers between devices: 33.2 us -> 0 us
  matrix products: 28 us -> 0 us
  blocking collectives: 21.6 us -> 0 us
  between operations: 15.5 us -> 0.64 us
  other arithmetic: 2.76 us -> 0 us
  local copies, waits for them, and re-layouts: 9.26 us -> 7.26 us
    pallas_call x0 -> x1, Pallas kernels: none -> 66.5 us  [per_device(): pl.pallas_call(functools.partial(kernel, n, na, tile, 1.0 / math.sqrt(uni...]
    all_gather x2 -> x0, waiting for transfers between devices: 31.8 us -> none  [the longest x1 31.8 us: per_device(): lax.all_gather(adapter_down, 'adapter', axis=0, tiled=True)]
    dot_general x3 -> x0, matrix products: 28 us -> none  [the longest x1 19.1 us: per_device(): product = jnp.dot(hidden, down_weight, preferred_element_type=jnp.float32)]
    psum x1 -> x0, blocking collectives: 21.6 us -> none  [per_device(): factor = lax.psum(factor.astype(jnp.bfloat16), 'mp').astype(jnp.float32)]
    gather x2 -> x0, local copies, waits for them, and re-layouts: 6.27 us -> none  [the longest x1 3.78 us: per_device(): moved_down = store_down[migration_plan]]
    unnamed x6 -> x3, local copies, waits for them, and re-layouts: 1.01 us -> 6.02 us
    convert_element_type x3 -> x0, other arithmetic: 2.75 us -> none  [the longest x1 2.74 us: per_device(): (base_product + low_rank_change.astype(jnp.float32)).astype(jnp.bfloat16)]
    convert_element_type x1 -> x0, local copies, waits for them, and re-layouts: 1.98 us -> none  [per_device(): base_product = lax.psum_scatter(jnp.transpose(product.reshape(row_count,...]
  transfers between devices with their start and end apart: 3 -> 0, of which waited for: 1 -> 0; matrix products, arithmetic and copies ran while one was open for 33% -> 0% of each run, Pallas kernels for 0% -> 0%
where the time goes in v1:
time: 74.6 us; the launch traced here: 74.4 us
  Pallas kernels  66.5 us (89%)
  local copies, waits for them, and re-layouts  7.26 us (10%)
    pallas_call x1, Pallas kernels, per_device(): pl.pallas_call(functools.partial(kernel, n, na, tile, 1.0 / math.sqrt(uni...  66.5 us
    unnamed x3, local copies, waits for them, and re-layouts  6.02 us

profile of v1, /device:TPU:0, one launch (start us, length us, event | category | flops | bytes accessed | tf_op | source)
XLA Modules:
  0.0 74.4 jit_solution(14553604689811865466)
XLA Ops:
  0.6 1.2 %broadcast_in_dim.3.ids_ref = s32[1,384]{1,0:T(1,128)} reshape(s32[384]{0:T(512)} %param.7) | data formatting | bytes 3072 | tf_op jit(solution)/shard_map/broadcast_in_dim | solution.py:314
  1.9 66.5 %shard_map.85 = (bf16[384,1024]{1,0:T(8,128)(2,1)}, bf16[2,64,4096]{2,1,0:T(8,128)(2,1)}, bf16[2,64,1024]{2,1,0:T(8,128)(2,1)}) custom-call(s32[2]{0:T(128)} %plan_ref.1, bf16[384,4096]{1,0:T(8,128)(2,1)} %hidden_ref.1, s32[1,384]{1,0:T(1,128)} %broadcast_in_dim.3.ids_ref, bf16[128,4096]{1,0:T(8,128)(2,1)} %bitcast.2, bf16[128,1024]{1,0:T(8,128)(2,1)} %bitcast.3, ...), custom_call_target="tpu_custom_call" | custom-call | tf_op jit(solution)/shard_map/pallas_call | solution.py:277
  68.4 2.1 %copy.12 = bf16[384,1024]{1,0:T(8,128)(2,1)} copy(bf16[384,1024]{1,0:T(8,128)(2,1)} %get-tuple-element.6) | data formatting | bytes 1572864
  70.4 2.3 %copy.13 = bf16[2,64,4096]{2,1,0:T(8,128)(2,1)} copy(bf16[2,64,4096]{2,1,0:T(8,128)(2,1)} %get-tuple-element.7) | data formatting | bytes 2097152
  72.7 1.7 %copy.14 = bf16[2,64,1024]{2,1,0:T(8,128)(2,1)} copy(bf16[2,64,1024]{2,1,0:T(8,128)(2,1)} %get-tuple-element.8) | data formatting | bytes 524288

commit v2 on v1

--- a/solution.py
+++ b/solution.py
@@ -15,9 +15,9 @@
 
 def kernel(
     n, na, tile, inv_units, out_scale,
-    plan_ref, hidden_ref, ids_ref, down_ref, up_ref, weight_ref,
+    plan_ref, ids_ref, hidden_hbm, down_ref, up_ref, weight_ref,
     out_ref, mdown_ref, mup_ref,
-    weights, prod, recv, store_down, store_up, fac, lora, spread, total,
+    weights, hidden_ref, prod, recv, store_down, store_up, fac, fac_in, fac_sum, lora, spread, total,
     w_sem, z_send, z_recv, local_sem, x_send, x_recv, f_send, f_recv,
 ):
     me = lax.axis_index("mp")
@@ -46,12 +46,12 @@
             weight_ref.at[:, pl.ds(col, tile)], weights.at[slot], w_sem.at[slot]
         )
 
+    own_hidden = pltpu.make_async_copy(hidden_hbm, hidden_ref, local_sem.at[2])
+    own_hidden.start()
     for t in range(SLOTS - 1):
         weight_copy(t, t).start()
     own_down = pltpu.make_async_copy(down_ref, store_down.at[ad], local_sem.at[0])
     own_up = pltpu.make_async_copy(up_ref, store_up.at[ad], local_sem.at[1])
-    own_down.start()
-    own_up.start()
 
     bits = []
     bit = na // 2
@@ -71,37 +71,39 @@
 
     barrier = pltpu.get_barrier_semaphore()
 
-    @pl.loop(1, n)
-    def _(i):
-        pl.semaphore_signal(
-            barrier, inc=1, device_id={"mp": (me + i) % n}, device_id_type=MESH
-        )
+    for here, step in ((before > 0, n - 1), (after > 0, 1)):
+
+        @pl.when(here)
+        def _(step=step):
+            pl.semaphore_signal(
+                barrier, inc=1, device_id={"mp": (me + step) % n}, device_id_type=MESH
+            )
 
     for b in bits:
         pl.semaphore_signal(
             barrier, inc=1, device_id={"adapter": partner(b)}, device_id_type=MESH
         )
-    pl.semaphore_wait(barrier, n - 1 + len(bits))
-
-    def adapter_copies(b, s):
+    pl.semaphore_wait(
+        barrier, (before > 0).astype(jnp.int32) + (after > 0).astype(jnp.int32) + len(bits)
+    )
+
+    def adapter_copy(i, b, s):
         slot = slot_of(s)
-        out = []
-        for i, (mine, store) in enumerate(((down_ref, store_down), (up_ref, store_up))):
-            out.append(
-                pltpu.make_async_remote_copy(
-                    src_ref=mine if s == 0 else store.at[slot],
-                    dst_ref=store.at[slot],
-                    send_sem=x_send.at[i, b ^ s],
-                    recv_sem=x_recv.at[i, b ^ s],
-                    device_id={"adapter": partner(b)},
-                    device_id_type=MESH,
-                )
-            )
-        return out
+        mine, store = ((down_ref, store_down), (up_ref, store_up))[i]
+        return pltpu.make_async_remote_copy(
+            src_ref=mine if s == 0 else store.at[slot],
+            dst_ref=store.at[slot],
+            send_sem=x_send.at[i, b ^ s],
+            recv_sem=x_recv.at[i, b ^ s],
+            device_id={"adapter": partner(b)},
+            device_id_type=MESH,
+        )
 
     for b in bits:
-        for c in adapter_copies(b, 0):
-            c.start()
+        adapter_copy(0, b, 0).start()
+    own_down.start()
+    own_up.start()
+    own_hidden.wait()
 
     def block_copy(d, right, j):
         return pltpu.make_async_remote_copy(
@@ -129,6 +131,7 @@
             ).astype(jnp.bfloat16)
             copy.start()
 
+    queued = (n - 1) * tiles - 3 * tiles // 4
     start_forward = tiles + 1
     early = max(0, min(-(-(count - start_forward) // STRIDE), (n - 2) * tiles))
 
@@ -147,7 +150,7 @@
             hidden_ref[...], weights[slot], preferred_element_type=jnp.float32
         ).astype(jnp.bfloat16)
 
-        @pl.when(jnp.logical_and(d != me, first_in_line(right)))
+        @pl.when((t < queued) & first_in_line(right))
         def _():
             block_copy(d, right, j).start()
 
@@ -162,64 +165,89 @@
     def _(i):
         forward(i)
 
-    held = [0]
-    for b in bits:
-        for s in held:
-            if s:
-                for c in adapter_copies(b, s):
-                    c.start()
-        if b == bits[-1]:
-
-            @pl.loop((n - 2) * tiles, (n - 1) * tiles)
-            def _(i):
-                forward(i)
-
-        for s in held:
-            for c in adapter_copies(b, s):
-                c.wait_recv()
-        held = held + [s ^ b for s in held]
-
+    def relay(i, before_last):
+        held = [0]
+        for b in bits:
+            for s in held:
+                if s:
+                    adapter_copy(i, b, s).start()
+            if b == bits[-1]:
+                before_last()
+            for s in held:
+                adapter_copy(i, b, s).wait_recv()
+            held = held + [s ^ b for s in held]
+
+    def rest():
+        for b in bits:
+            adapter_copy(1, b, 0).start()
+
+        @pl.loop((n - 2) * tiles, (n - 1) * tiles)
+        def _(i):
+            forward(i)
+
+    relay(0, rest)
     own_down.wait()
-    own_up.wait()
 
     total_adapters = na * local_count
     stacked = store_down[...].reshape(total_adapters * rank, store_down.shape[2])
     every = lax.dot_general(
         stacked, hidden_ref[...], (((1,), (1,)), ((), ())), preferred_element_type=jnp.float32
     )
-    ids = ids_ref[...]
+    ids = ids_ref[...].reshape(1, rows)
     part = jnp.zeros((rank, rows), jnp.float32)
     for g in range(total_adapters):
         part = part + jnp.where(ids == g, every[g * rank : (g + 1) * rank], 0.0)
-    fac[me] = part.astype(jnp.bfloat16)
-
-    def factor_copy(source, target):
+
+    def factor_copy(right):
         return pltpu.make_async_remote_copy(
-            src_ref=fac.at[source],
-            dst_ref=fac.at[source],
-            send_sem=f_send.at[target],
-            recv_sem=f_recv.at[source],
-            device_id={"mp": target},
+            src_ref=fac.at[right],
+            dst_ref=fac_in.at[right],
+            send_sem=f_send.at[right],
+            recv_sem=f_recv.at[right],
+            device_id={"mp": (me + 1) % n if right else (me + n - 1) % n},
             device_id_type=MESH,
         )
 
-    @pl.loop(1, n)
+    mine = part.astype(jnp.bfloat16)
+    fac[0] = mine
+    fac[1] = mine
+    ends = ((1, before, after), (0, after, before))
+    for right, upstream, _ in ends:
+
+        @pl.when(upstream == 0)
+        def _(right=right):
+            factor_copy(right).start()
+
+    @pl.loop(queued, (n - 1) * tiles)
     def _(i):
-        factor_copy(me, (me + i) % n).start()
-
+        d, right = visit(i // tiles)
+
+        @pl.when(first_in_line(right))
+        def _():
+            block_copy(d, right, i % tiles).start()
+
+    relay(1, lambda: None)
+    own_up.wait()
     for s in range(local_count):
         g = plan_ref[s]
         mdown_ref[s] = store_down[g // local_count, pl.ds((g % local_count) * rank, rank), :]
         mup_ref[s] = store_up[g // local_count, pl.ds((g % local_count) * rank, rank), :]
 
-    @pl.loop(1, n)
-    def _(i):
-        other = (me + i) % n
-        factor_copy(other, other).wait_recv()
-
-    factor = fac[0].astype(jnp.float32)
-    for i in range(1, n):
-        factor = factor + fac[i].astype(jnp.float32)
+    fac_sum[...] = part
+    for right, upstream, downstream in ends:
+
+        @pl.when(upstream > 0)
+        def _(right=right, downstream=downstream):
+            factor_copy(right).wait_recv()
+            came = fac_in[right].astype(jnp.float32)
+            fac_sum[...] += came
+
+            @pl.when(downstream > 0)
+            def _():
+                fac[right] = (fac[right].astype(jnp.float32) + came).astype(jnp.bfloat16)
+                factor_copy(right).start()
+
+    factor = fac_sum[...]
     factor = (factor * inv_units).astype(jnp.bfloat16).astype(jnp.float32)
     for g in range(total_adapters):
         spread[g * rank : (g + 1) * rank, :] = jnp.where(ids == g, factor, 0.0).astype(
@@ -254,16 +282,27 @@
         d, right = visit(i // tiles)
         block_copy(d, right, i % tiles).wait_send()
 
-    @pl.loop(1, n)
-    def _(i):
-        factor_copy(me, (me + i) % n).wait_send()
+    for right, _, downstream in ends:
+
+        @pl.when(downstream > 0)
+        def _(right=right):
+            factor_copy(right).wait_send()
 
     held = [0]
     for b in bits:
         for s in held:
-            for c in adapter_copies(b, s):
-                c.wait_send()
+            for i in range(2):
+                adapter_copy(i, b, s).wait_send()
         held = held + [s ^ b for s in held]
+
+
+def place(*refs):
+    sources, targets, sems = refs[:3], refs[3:6], refs[6]
+    copies = [pltpu.make_async_copy(a, b, sems.at[i]) for i, (a, b) in enumerate(zip(sources, targets))]
+    for c in copies:
+        c.start()
+    for c in copies:
+        c.wait()
 
 
 def per_device(n, na, hidden, adapter_ids, down_weight, adapter_down, adapter_up, migration_plan):
@@ -273,50 +312,60 @@
     tiles = width // tile
     stack = local_count * rank
     vmem = pl.BlockSpec(memory_space=pltpu.VMEM)
+    anywhere = pl.BlockSpec(memory_space=pl.ANY)
     bf16 = jnp.bfloat16
-    result, moved_down, moved_up = pl.pallas_call(
+    shapes = (
+        jax.ShapeDtypeStruct((rows, width), bf16),
+        jax.ShapeDtypeStruct(adapter_down.shape, bf16),
+        jax.ShapeDtypeStruct(adapter_up.shape, bf16),
+    )
+    held = pl.pallas_call(
         functools.partial(
             kernel, n, na, tile, 1.0 / math.sqrt(units * n), 0.5 / math.sqrt(rank)
         ),
-        out_shape=(
-            jax.ShapeDtypeStruct((rows, width), bf16),
-            jax.ShapeDtypeStruct(adapter_down.shape, bf16),
-            jax.ShapeDtypeStruct(adapter_up.shape, bf16),
-        ),
-        in_specs=[pl.BlockSpec(memory_space=pltpu.SMEM), vmem, vmem, vmem, vmem]
-        + [pl.BlockSpec(memory_space=pl.ANY)],
+        out_shape=tuple(pltpu.VMEM(x.shape, x.dtype) for x in shapes),
+        in_specs=[pl.BlockSpec(memory_space=pltpu.SMEM), vmem] + [anywhere] * 4,
         out_specs=(vmem, vmem, vmem),
         scratch_shapes=[
             pltpu.VMEM((SLOTS, units, tile), bf16),
+            pltpu.VMEM((rows, units), bf16),
             pltpu.VMEM((n, tiles, rows, tile), bf16),
             pltpu.VMEM((2, n, tiles, rows, tile), bf16),
             pltpu.VMEM((na, stack, units), bf16),
             pltpu.VMEM((na, stack, width), bf16),
-            pltpu.VMEM((n, rank, rows), bf16),
+            pltpu.VMEM((2, rank, rows), bf16),
+            pltpu.VMEM((2, rank, rows), bf16),
+            pltpu.VMEM((rank, rows), jnp.float32),
             pltpu.VMEM((rows, width), bf16),
             pltpu.VMEM((na * stack, rows), bf16),
             pltpu.VMEM((rows, tile), jnp.float32),
             pltpu.SemaphoreType.DMA((SLOTS,)),
             pltpu.SemaphoreType.DMA((n, tiles)),
             pltpu.SemaphoreType.DMA((2, n, tiles)),
-            pltpu.SemaphoreType.DMA((2,)),
+            pltpu.SemaphoreType.DMA((3,)),
             pltpu.SemaphoreType.DMA((2, na)),
             pltpu.SemaphoreType.DMA((2, na)),
-            pltpu.SemaphoreType.DMA((n,)),
-            pltpu.SemaphoreType.DMA((n,)),
+            pltpu.SemaphoreType.DMA((2,)),
+            pltpu.SemaphoreType.DMA((2,)),
         ],
         compiler_params=pltpu.CompilerParams(
             collective_id=0, has_side_effects=True, vmem_limit_bytes=56 << 20
         ),
     )(
         migration_plan,
+        adapter_ids,
         hidden,
-        adapter_ids[None, :],
         adapter_down.reshape(stack, units),
         adapter_up.reshape(stack, width),
         down_weight,
     )
-    return result, moved_down, moved_up
+    return pl.pallas_call(
+        place,
+        out_shape=shapes,
+        in_specs=[vmem] * 3,
+        out_specs=(anywhere,) * 3,
+        scratch_shapes=[pltpu.SemaphoreType.DMA((3,))],
+    )(*(pltpu.with_memory_space_constraint(x, pltpu.VMEM) for x in held))
 
 
 def solution(mesh):

time: 74.6 us -> 61.2 us (0.82)
  the two profiles are of different devices: /device:TPU:0 before, /device:TPU:18 now
where the time goes in v2:
time: 61.2 us; the launch traced here: 61.1 us
  Pallas kernels  60.4 us (99%)
  between operations  0.64 us (1%)
    pallas_call x1, Pallas kernels, per_device(): pl.pallas_call(functools.partial(kernel, n, na, tile, 1.0 / math.sqrt(uni...  59.1 us
    pallas_call x1, Pallas kernels, per_device(): pl.pallas_call(place, out_shape=shapes, in_specs=[vmem] * 3, out_specs=(a...  1.34 us

profile of v2, /device:TPU:18, one launch (start us, length us, event | category | flops | bytes accessed | tf_op | source)
XLA Modules:
  0.0 61.1 jit_solution(5603070433086596967)
XLA Ops:
  0.6 59.1 %shard_map.85 = (bf16[384,1024]{1,0:T(8,128)(2,1)S(1)}, bf16[2,64,4096]{2,1,0:T(8,128)(2,1)S(1)}, bf16[2,64,1024]{2,1,0:T(8,128)(2,1)S(1)}) custom-call(s32[2]{0:T(128)} %plan_ref.1, s32[384]{0:T(512)} %ids_ref.1, bf16[384,4096]{1,0:T(8,128)(2,1)} %hidden_hbm.1, bf16[128,4096]{1,0:T(8,128)(2,1)} %bitcast.2, bf16[128,1024]{1,0:T(8,128)(2,1)} %bitcast.3, ...), custom_call_target="tpu_custom_call" | custom-call | tf_op jit(solution)/shard_map/pallas_call | solution.py:322
  59.7 1.3 %shard_map.86 = (bf16[384,1024]{1,0:T(8,128)(2,1)}, bf16[2,64,4096]{2,1,0:T(8,128)(2,1)}, bf16[2,64,1024]{2,1,0:T(8,128)(2,1)}) custom-call(bf16[384,1024]{1,0:T(8,128)(2,1)S(1)} %get-tuple-element.6.refs_0_, bf16[2,64,4096]{2,1,0:T(8,128)(2,1)S(1)} %get-tuple-element.7.refs_1_, bf16[2,64,1024]{2,1,0:T(8,128)(2,1)S(1)} %get-tuple-element.8.refs_2_), custom_call_target="tpu_custom_call" | custom-call | tf_op jit(solution)/shard_map/pallas_call | solution.py:362

commit v3 on v2

--- a/solution.py
+++ b/solution.py
@@ -228,15 +228,12 @@
 
     relay(1, lambda: None)
     own_up.wait()
-    for s in range(local_count):
-        g = plan_ref[s]
-        mdown_ref[s] = store_down[g // local_count, pl.ds((g % local_count) * rank, rank), :]
-        mup_ref[s] = store_up[g // local_count, pl.ds((g % local_count) * rank, rank), :]
-
     fac_sum[...] = part
-    for right, upstream, downstream in ends:
-
-        @pl.when(upstream > 0)
+    for right, upstream, downstream, here in (
+        (*ends[0], before < after), (*ends[1], before >= 0), (*ends[0], before >= after)
+    ):
+
+        @pl.when((upstream > 0) & here)
         def _(right=right, downstream=downstream):
             factor_copy(right).wait_recv()
             came = fac_in[right].astype(jnp.float32)
@@ -264,6 +261,11 @@
             )
             * out_scale
         ).astype(jnp.bfloat16)
+
+    for s in range(local_count):
+        g = plan_ref[s]
+        mdown_ref[s] = store_down[g // local_count, pl.ds((g % local_count) * rank, rank), :]
+        mup_ref[s] = store_up[g // local_count, pl.ds((g % local_count) * rank, rank), :]
 
     for j in range(tiles):
         cols = slice(j * tile, (j + 1) * tile)

time: 61.2 us -> 61.3 us (level)
  no operation moved by 1% of the time
where the time goes in v3:
time: 61.3 us; the launch traced here: 61.1 us
  Pallas kernels  60.4 us (99%)
  between operations  0.64 us (1%)
    pallas_call x1, Pallas kernels, per_device(): pl.pallas_call(functools.partial(kernel, n, na, tile, 1.0 / math.sqrt(uni...  59.1 us
    pallas_call x1, Pallas kernels, per_device(): pl.pallas_call(place, out_shape=shapes, in_specs=[vmem] * 3, out_specs=(a...  1.34 us

profile of v3, /device:TPU:18, one launch (start us, length us, event | category | flops | bytes accessed | tf_op | source)
XLA Modules:
  0.0 61.1 jit_solution(14947046278976097895)
XLA Ops:
  0.6 59.1 %shard_map.85 = (bf16[384,1024]{1,0:T(8,128)(2,1)S(1)}, bf16[2,64,4096]{2,1,0:T(8,128)(2,1)S(1)}, bf16[2,64,1024]{2,1,0:T(8,128)(2,1)S(1)}) custom-call(s32[2]{0:T(128)} %plan_ref.1, s32[384]{0:T(512)} %ids_ref.1, bf16[384,4096]{1,0:T(8,128)(2,1)} %hidden_hbm.1, bf16[128,4096]{1,0:T(8,128)(2,1)} %bitcast.2, bf16[128,1024]{1,0:T(8,128)(2,1)} %bitcast.3, ...), custom_call_target="tpu_custom_call" | custom-call | tf_op jit(solution)/shard_map/pallas_call | solution.py:324
  59.8 1.3 %shard_map.86 = (bf16[384,1024]{1,0:T(8,128)(2,1)}, bf16[2,64,4096]{2,1,0:T(8,128)(2,1)}, bf16[2,64,1024]{2,1,0:T(8,128)(2,1)}) custom-call(bf16[384,1024]{1,0:T(8,128)(2,1)S(1)} %get-tuple-element.6.refs_0_, bf16[2,64,4096]{2,1,0:T(8,128)(2,1)S(1)} %get-tuple-element.7.refs_1_, bf16[2,64,1024]{2,1,0:T(8,128)(2,1)S(1)} %get-tuple-element.8.refs_2_), custom_call_target="tpu_custom_call" | custom-call | tf_op jit(solution)/shard_map/pallas_call | solution.py:364
